TPU v7x, 32 devices: a whole 2x2x4 slice. The times are simulated.
32 devices in a mesh: prow: 8 (over z, x), pcol: 4 (over y, core).
Axes of the slice: x: 2, y: 2, z: 4, core: 2. Of those that a mesh axis runs over, the one named last changes fastest.
Arguments:
- system: bfloat16 [6144, 65536], P('prow', 'pcol'), may hold values from -6 to 6
- row_outer: float32 [6144], P('prow'), may hold values from 0.5 to 2
- row_inner: float32 [6144], P('prow'), may hold values from 0.5 to 2
- col_outer: float32 [65536], P('pcol'), may hold values from 0.5 to 2
- col_inner: float32 [65536], P('pcol'), may hold values from 0.5 to 2
- diag_inverse: bfloat16 [512, 512], replicated, may hold values from -0.01171875 to 0.01171875
Outputs:
- trailing: bfloat16 [6144, 65536], P('prow', 'pcol')
All inputs are finite; a program needn't handle non-finite values.
Results may differ from a plain program's by a relative error of at most 0.0089.
Values may be sent and summed in bfloat16 or wider, within the bound.
A program may use at most 192 MiB of HBM per device.

v0:
```python
import jax
import jax.numpy as jnp
from jax import lax
from jax.sharding import PartitionSpec as P

root_half = 0.7071067811865476


def partner_2(block, axis, stride):
    count = lax.axis_size(axis)
    route = []
    for low in range(count):
        high = low | 1 << stride
        if high != low and high < count:
            route += [(low, high), (high, low)]
    return lax.ppermute(block, axis, route)


def from_root(block, axis, owner):
    block = jnp.where(lax.axis_index(axis) == owner, block, jnp.zeros_like(block))
    return lax.psum(block, axis)


def combine(values, partner, weights, upper):
    mine = values.astype(jnp.float32)
    other = partner.astype(jnp.float32)
    summed = jnp.where(upper, mine + other, other - mine)
    return (weights * summed * root_half).astype(jnp.bfloat16)


def per_device(system, row_outer, row_inner, col_outer, col_inner, diag_inverse):
    panel = diag_inverse.shape[0]
    rows_here = system.shape[0]
    row_bits = lax.axis_size("prow").bit_length() - 1
    col_bits = lax.axis_size("pcol").bit_length() - 1
    row_place = lax.axis_index("prow")
    col_place = lax.axis_index("pcol")
    partner = partner_2(system, "prow", row_bits - 1)
    first = combine(system, partner, row_outer[:, None], row_place >> row_bits - 1 & 1 == 0)
    partner = partner_2(first, "prow", row_bits - 2)
    second = combine(first, partner, row_inner[:, None], row_place >> row_bits - 2 & 1 == 0)
    partner = partner_2(second, "pcol", col_bits - 1)
    third = combine(second, partner, col_outer[None, :], col_place >> col_bits - 1 & 1 == 0)
    partner = partner_2(third, "pcol", col_bits - 2)
    transformed = combine(third, partner, col_inner[None, :], col_place >> col_bits - 2 & 1 == 0)
    leading = transformed[:, :panel]
    received = from_root(leading, "pcol", 0)
    left = jnp.dot(received, diag_inverse, preferred_element_type=jnp.float32).astype(jnp.bfloat16)
    taken = min(rows_here, panel)
    pieces = from_root(transformed[:taken], "prow", 0)
    update = jnp.dot(left, pieces, preferred_element_type=jnp.float32)
    return (transformed.astype(jnp.float32) - update).astype(jnp.bfloat16)


def solution(mesh):
    in_specs = (P("prow", "pcol"), P("prow"), P("prow"), P("pcol"), P("pcol"), P())
    out_specs = P("prow", "pcol")
    return jax.shard_map(
        per_device, mesh=mesh, in_specs=in_specs, out_specs=out_specs, check_vma=False
    )
```

profile of v0, /device:TPU:7, one launch (start us, length us, event | category | flops | bytes accessed | tf_op | source)
XLA Modules:
  0.0 2915.1 jit_solution(8006526509726187946)
XLA Ops:
  6.5 0.0 copy-start
  6.5 0.0 all-reduce.3.cloned.1.call-start
  6.5 2.3 collective-permute-start
  8.8 0.0 copy-start.3
  8.9 1079.1 %collective-permute-done = bf16[768,16384]{1,0:T(8,128)(2,1)} collective-permute-done((bf16[768,16384]{1,0:T(8,128)(2,1)}, bf16[768,16384]{1,0:T(8,128)(2,1)}, u32[]{:S(2)}, u32[]{:S(2)}) %collective-permute-start) | collective-permute-done | bytes 25165856 | tf_op jit(solution)/shard_map/ppermute | solution.py:16
  1087.9 29.8 %fusion.3 = bf16[768,16384]{1,0:T(8,128)(2,1)} fusion(bf16[768,16384]{1,0:T(8,128)(2,1)} %collective-permute-done, bf16[768,16384]{1,0:T(8,128)(2,1)} %param.6, f32[768]{0:T(1024)} %param.7, pred[]{:T(512)S(6)} %eq.21), kind=kLoop, calls=%fused_computation.11 | loop fusion | flops 100663296 | bytes 75500544 | tf_op jit(solution)/shard_map/convert_element_type | solution.py:28
  1117.8 1.4 collective-permute-start.1
  1119.2 0.0 copy-start.1
  1119.2 539.2 %collective-permute-done.1 = bf16[768,16384]{1,0:T(8,128)(2,1)} collective-permute-done((bf16[768,16384]{1,0:T(8,128)(2,1)}, bf16[768,16384]{1,0:T(8,128)(2,1)}, u32[]{:S(2)}, u32[]{:S(2)}) %collective-permute-start.1) | collective-permute-done | bytes 25165856 | tf_op jit(solution)/shard_map/ppermute | solution.py:16
  1658.4 0.0 copy-done.3
  1658.4 29.8 %fusion.7 = bf16[768,16384]{1,0:T(8,128)(2,1)} fusion(bf16[768,16384]{1,0:T(8,128)(2,1)} %collective-permute-done.1, bf16[768,16384]{1,0:T(8,128)(2,1)} %fusion.3, f32[768]{0:T(1024)S(1)} %copy-done.3, pred[]{:T(512)S(6)} %eq.20), kind=kLoop, calls=%fused_computation.15 | loop fusion | flops 100663296 | bytes 75500544 | tf_op jit(solution)/shard_map/convert_element_type | solution.py:28
  1688.2 0.2 collective-permute-start.2
  1688.4 0.0 copy-start.2
  1688.4 539.5 %collective-permute-done.2 = bf16[768,16384]{1,0:T(8,128)(2,1)} collective-permute-done((bf16[768,16384]{1,0:T(8,128)(2,1)}, bf16[768,16384]{1,0:T(8,128)(2,1)}, u32[]{:S(2)}, u32[]{:S(2)}) %collective-permute-start.2) | collective-permute-done | bytes 25165856 | tf_op jit(solution)/shard_map/ppermute | solution.py:16
  2227.9 0.0 copy-done.1
  2227.9 29.8 %fusion.11 = bf16[768,16384]{1,0:T(8,128)(2,1)} fusion(bf16[768,16384]{1,0:T(8,128)(2,1)} %collective-permute-done.2, bf16[768,16384]{1,0:T(8,128)(2,1)} %fusion.7, f32[16384]{0:T(1024)S(1)} %copy-done.1, pred[]{:T(512)S(6)} %eq.19), kind=kLoop, calls=%fused_computation.19 | loop fusion | flops 100663296 | bytes 75563008 | tf_op jit(solution)/shard_map/convert_element_type | solution.py:28
  2257.7 3.0 collective-permute-start.3
  2260.7 37.1 %collective-permute-done.3 = bf16[768,16384]{1,0:T(8,128)(2,1)} collective-permute-done((bf16[768,16384]{1,0:T(8,128)(2,1)}, bf16[768,16384]{1,0:T(8,128)(2,1)}, u32[]{:S(2)}, u32[]{:S(2)}) %collective-permute-start.3) | collective-permute-done | bytes 25165856 | tf_op jit(solution)/shard_map/ppermute | solution.py:16
  2297.8 0.0 copy-done.2
  2297.8 29.8 %fusion.15 = bf16[768,16384]{1,0:T(8,128)(2,1)} fusion(bf16[768,16384]{1,0:T(8,128)(2,1)} %collective-permute-done.3, bf16[768,16384]{1,0:T(8,128)(2,1)} %fusion.11, f32[16384]{0:T(1024)S(1)} %copy-done.2, pred[]{:T(512)S(6)} %eq.18), kind=kLoop, calls=%fused_computation.23 | loop fusion | flops 100663296 | bytes 75563008 | tf_op jit(solution)/shard_map/convert_element_type | solution.py:28
  2327.6 2.1 slice_select_fusion.1
  2329.7 0.0 all-reduce.3.cloned.1.call-update
  2329.7 0.0 all-reduce.5.cloned.1.call-start
  2329.8 13.8 slice_select_fusion
  2343.5 0.0 all-reduce.5.cloned.1.call-update
  2343.6 22.3 all-reduce.3.cloned.1.call-done
  2365.9 515.4 %all-reduce.5.cloned.1.call-done = bf16[512,16384]{1,0:T(8,128)(2,1)} async-done(((bf16[512,16384]{1,0:T(8,128)(2,1)}), bf16[512,16384]{1,0:T(8,128)(2,1)}) %all-reduce.5.cloned.1.call-update) | async-done | bytes 16777232 | tf_op jit(solution)/shard_map/psum | solution.py:21
  2881.3 0.0 copy-done
  2881.3 27.0 subtract_convert_fusion
Async XLA Ops:
  6.5 2874.7 %copy-start = (bf16[512,512]{1,0:T(8,128)(2,1)S(1)}, bf16[512,512]{1,0:T(8,128)(2,1)}, u32[]{:S(2)}) copy-start(bf16[512,512]{1,0:T(8,128)(2,1)} %param.11) | copy-start | bytes 1572868
  6.5 2359.3 %all-reduce.3.cloned.1.call-start = ((), (), s32[]{:S(2)}) async-start(), calls=%async_computation | async-start | bytes 1572864 | tf_op jit(solution)/shard_map/psum | solution.py:21
  6.5 1081.4 %collective-permute-start = (bf16[768,16384]{1,0:T(8,128)(2,1)}, bf16[768,16384]{1,0:T(8,128)(2,1)}, u32[]{:S(2)}, u32[]{:S(2)}) collective-permute-start(bf16[768,16384]{1,0:T(8,128)(2,1)} %param.6), channel_id=1, source_target_pairs={{0,16},{16,0},{4,20},{20,4},{8,24},{24,8},{12,28},{28,12},{1,17},{... | collective-permute-start | bytes 75497480 | tf_op jit(solution)/shard_map/ppermute | solution.py:16
  8.8 1649.5 %copy-start.3 = (f32[768]{0:T(1024)S(1)}, f32[768]{0:T(1024)}, u32[]{:S(2)}) copy-start(f32[768]{0:T(1024)} %param.8) | copy-start | bytes 9220
  1117.8 540.6 %collective-permute-start.1 = (bf16[768,16384]{1,0:T(8,128)(2,1)}, bf16[768,16384]{1,0:T(8,128)(2,1)}, u32[]{:S(2)}, u32[]{:S(2)}) collective-permute-start(bf16[768,16384]{1,0:T(8,128)(2,1)} %fusion.3), channel_id=1, source_target_pairs={{0,8},{8,0},{4,12},{12,4},{16,24},{24,16},{20,28},{28,20},{1,9},{9... | collective-permute-start | bytes 75497480 | tf_op jit(solution)/shard_map/ppermute | solution.py:16
  1119.2 1108.7 %copy-start.1 = (f32[16384]{0:T(1024)S(1)}, f32[16384]{0:T(1024)}, u32[]{:S(2)}) copy-start(f32[16384]{0:T(1024)} %param.9) | copy-start | bytes 196612
  1688.2 539.7 %collective-permute-start.2 = (bf16[768,16384]{1,0:T(8,128)(2,1)}, bf16[768,16384]{1,0:T(8,128)(2,1)}, u32[]{:S(2)}, u32[]{:S(2)}) collective-permute-start(bf16[768,16384]{1,0:T(8,128)(2,1)} %fusion.7), channel_id=1, source_target_pairs={{0,2},{2,0},{1,3},{3,1},{4,6},{6,4},{5,7},{7,5},{8,10},{10,8},{9,1... | collective-permute-start | bytes 75497480 | tf_op jit(solution)/shard_map/ppermute | solution.py:16
  1688.4 609.4 %copy-start.2 = (f32[16384]{0:T(1024)S(1)}, f32[16384]{0:T(1024)}, u32[]{:S(2)}) copy-start(f32[16384]{0:T(1024)} %param.10) | copy-start | bytes 196612
  2257.7 40.1 %collective-permute-start.3 = (bf16[768,16384]{1,0:T(8,128)(2,1)}, bf16[768,16384]{1,0:T(8,128)(2,1)}, u32[]{:S(2)}, u32[]{:S(2)}) collective-permute-start(bf16[768,16384]{1,0:T(8,128)(2,1)} %fusion.11), channel_id=1, source_target_pairs={{0,1},{1,0},{2,3},{3,2},{4,5},{5,4},{6,7},{7,6},{8,9},{9,8},{10,11... | collective-permute-start | bytes 75497480 | tf_op jit(solution)/shard_map/ppermute | solution.py:16
  2329.7 551.5 %all-reduce.5.cloned.1.call-start = ((), (), s32[]{:S(2)}) async-start(), calls=%async_computation.1 | async-start | bytes 33554432 | tf_op jit(solution)/shard_map/psum | solution.py:21
Sparse Core Ops, SparseCore 0:
  2329.8 35.9 all-reduce.2
  2370.0 511.2 all-reduce.4
where the time goes:
time: 2920 us
  waiting for transfers between devices  2730 us (93%)
  other arithmetic  135 us (5%)
    ppermute x4, waiting for transfers between devices, partner_2(): return lax.ppermute(block, axis, route)  2190 us
    psum x2, waiting for transfers between devices, from_root(): return lax.psum(block, axis)  538 us
    convert_element_type x4, other arithmetic, combine(): return (weights * summed * root_half).astype(jnp.bfloat16)  119 us
  transfers between devices with their start and end apart: 6, of which 6 were waited for; matrix products, arithmetic and copies ran while one was open for 0% of the time, Pallas kernels for 0%

commit v1 on v0

v1 whole, which is shorter than its diff:
```python
import functools

import jax
import jax.numpy as jnp
from jax import lax
from jax.experimental import pallas as pl
from jax.experimental.pallas import tpu as pltpu
from jax.sharding import PartitionSpec as P

root_half = 0.7071067811865476
MESH = pl.DeviceIdType.MESH
WIDTH = 512
STRIP = 32
SLOTS = 4
LAST = 5


def kernel(
    K, width, panel, R, Q,
    system, row_coef, col_coef,
    full, lead, leading,
    s_buf, ra, tb, rb, m_buf, rc, rd1, rd2, e_buf, k_buf, l_buf,
    load_sem, a_send, a_recv, b_send, b_recv, m_send, c_recv, d1_recv, d2_send, d2_recv,
    e_send, e_recv, l_send, l_recv, k_sem, lk_sem, f_send, f_recv, g_send, g_recv,
    cred_a, cred_b, cred_c, cred_d,
):
    rows = system.shape[0]
    C = Q // 4
    prow = lax.axis_index("prow")
    pcol = lax.axis_index("pcol")
    quarter = prow // R
    rank = prow % R
    col_quarter = pcol // C
    inner = (quarter == 1) | (quarter == 2)
    outer = (quarter == 0) | (quarter == 3)
    first_rank = rank == 0

    y_dev = (prow, lax.rem(pcol + 2 * C, Q))
    core_dev = (prow, jnp.where(col_quarter % 2 == 0, pcol + C, pcol - C))
    edge_dev = (jnp.where(quarter % 2 == 0, prow + R, prow - R), pcol)
    mid_dev = ((3 - quarter) * R + rank, pcol)

    def signal(sem, device):
        pl.semaphore_signal(sem, inc=1, device_id=device, device_id_type=MESH)

    barrier = pltpu.get_barrier_semaphore()
    for d in range(1, Q):
        signal(barrier, (prow, lax.rem(pcol + d, Q)))
    for d in range(1, R):
        signal(barrier, (quarter * R + lax.rem(rank + d, R), pcol))
    signal(barrier, edge_dev)
    signal(barrier, mid_dev)
    pl.semaphore_wait(barrier, Q - 1 + R - 1 + 2)

    def at(c):
        return pl.ds(pl.multiple_of(c * width, width), width)

    def remote(src, dst, send, recv, device):
        return pltpu.make_async_remote_copy(
            src_ref=src, dst_ref=dst, send_sem=send, recv_sem=recv, device_id=device, device_id_type=MESH
        )

    def load(c):
        return pltpu.make_async_copy(system.at[:, at(c)], s_buf.at[c % SLOTS], load_sem.at[c % SLOTS])

    def a_copy(c):
        k = c % SLOTS
        return remote(s_buf.at[k], ra.at[k], a_send.at[k], a_recv.at[k], y_dev)

    def b_copy(c):
        k = c % 2
        return remote(tb.at[k], rb.at[k], b_send.at[k], b_recv.at[k], core_dev)

    def c_copy(c):
        k = c % SLOTS
        return remote(m_buf.at[k], rc.at[k], m_send.at[k], c_recv.at[k], edge_dev)

    def d1_copy(c):
        k = c % SLOTS
        return remote(m_buf.at[k], rd1.at[k], m_send.at[k], d1_recv.at[k], mid_dev)

    def d2_copy(c):
        k = c % SLOTS
        return remote(rc.at[k], rd2.at[k], d2_send.at[k], d2_recv.at[k], mid_dev)

    def e_copy(c):
        k = c % 2
        return remote(e_buf.at[k], full.at[:, at(c)], e_send.at[k], e_recv.at[c], edge_dev)

    def l_copy(c):
        k = c % 2
        return remote(l_buf.at[k], lead.at[:, at(c)], l_send.at[k], l_recv.at[c], edge_dev)

    def k_copy(c):
        return pltpu.make_async_copy(k_buf.at[c % 2], full.at[:, at(c)], k_sem.at[c % 2])

    def lk_copy(c):
        return pltpu.make_async_copy(l_buf.at[c % 2], lead.at[:, at(c)], lk_sem.at[c % 2])

    def f_copy(c, d, from_hbm):
        src = lead.at[:, at(c)] if from_hbm else l_buf.at[c % 2]
        return remote(src, lead.at[:, at(c)], f_send.at[c % 2, d - 1], f_recv.at[c], (quarter * R + d, pcol))

    def g_copy(d):
        return remote(full.at[:, pl.ds(0, panel)], leading, g_send.at[d - 1], g_recv.at[0], (prow, d))

    def mix(mine, got, out, c, which):
        u = col_coef[which : which + 1, at(c)]
        v = col_coef[which + 1 : which + 2, at(c)]

        @pl.loop(0, rows // STRIP)
        def _(j):
            r = pl.ds(pl.multiple_of(j * STRIP, STRIP), STRIP)
            x = mine[r, :].astype(jnp.float32)
            y = got[r, :].astype(jnp.float32)
            out[r, :] = (u * x + v * y).astype(jnp.bfloat16)

    def combine(k, outs, strips):
        @pl.loop(0, strips)
        def _(j):
            r = pl.ds(pl.multiple_of(j * STRIP, STRIP), STRIP)
            w = row_coef[r, :]
            o = m_buf[k, r, :].astype(jnp.float32)
            n = rc[k, r, :].astype(jnp.float32)
            a = rd1[k, r, :].astype(jnp.float32)
            f = rd2[k, r, :].astype(jnp.float32)
            for out, b in outs:
                total = w[:, b : b + 1] * o + w[:, b + 1 : b + 2] * n
                total += w[:, b + 2 : b + 3] * a + w[:, b + 3 : b + 4] * f
                out[r, :] = total.astype(jnp.bfloat16)

    for c in range(3):
        load(c).start()
    for c in range(2):
        load(c).wait()
        a_copy(c).start()

    def body(i, carry):
        @pl.when(i + 3 < K)
        def _():
            load(i + 3).start()

        @pl.when(i + 2 < K)
        def _():
            c = i + 2
            load(c).wait()

            @pl.when(c >= SLOTS)
            def _():
                pl.semaphore_wait(cred_a, 1)

            a_copy(c).start()

        @pl.when(i < K)
        def _():
            c = i
            a_copy(c).wait_recv()

            @pl.when(c >= 2)
            def _():
                b_copy(c - 2).wait_send()

            mix(s_buf.at[c % SLOTS], ra.at[c % SLOTS], tb.at[c % 2], c, 0)
            a_copy(c).wait_send()

            @pl.when(c + SLOTS < K)
            def _():
                signal(cred_a, y_dev)

            @pl.when(c >= 2)
            def _():
                pl.semaphore_wait(cred_b, 1)

            b_copy(c).start()
            b_copy(c).wait_recv()

            @pl.when(outer & (c >= SLOTS))
            def _():
                c_copy(c - SLOTS).wait_send()

            mix(tb.at[c % 2], rb.at[c % 2], m_buf.at[c % SLOTS], c, 2)

            @pl.when(c + 2 < K)
            def _():
                signal(cred_b, core_dev)

            @pl.when(outer)
            def _():
                @pl.when(c >= SLOTS)
                def _():
                    pl.semaphore_wait(cred_c, 1)

                c_copy(c).start()

            @pl.when(inner)
            def _():
                @pl.when(c >= SLOTS)
                def _():
                    pl.semaphore_wait(cred_d, 1)

                d1_copy(c).start()

        @pl.when(inner & (i >= 1) & (i - 1 < K))
        def _():
            c = i - 1
            c_copy(c).wait_recv()
            d2_copy(c).start()

        @pl.when(inner & (i >= 3) & (i - 3 < K))
        def _():
            c = i - 3
            d1_copy(c).wait()
            d2_copy(c).wait()

            @pl.when(c >= 2)
            def _():
                e_copy(c - 2).wait_send()
                k_copy(c - 2).wait()

            combine(c % SLOTS, ((e_buf.at[c % 2], 0), (k_buf.at[c % 2], 4)), rows // STRIP)
            e_copy(c).start()
            k_copy(c).start()

            @pl.when(first_rank)
            def _():
                @pl.when(c >= 2)
                def _():
                    l_copy(c - 2).wait_send()
                    lk_copy(c - 2).wait()
                    for d in range(1, R):
                        f_copy(c - 2, d, False).wait_send()

                combine(c % SLOTS, ((l_buf.at[c % 2], 8),), panel // STRIP)
                l_copy(c).start()
                lk_copy(c).start()
                for d in range(1, R):
                    f_copy(c, d, False).start()

            @pl.when(c + SLOTS < K)
            def _():
                signal(cred_c, edge_dev)
                signal(cred_d, mid_dev)

        @pl.when(outer & (i >= LAST) & (i - LAST < K))
        def _():
            c = i - LAST
            e_copy(c).wait_recv()

            @pl.when(first_rank)
            def _():
                l_copy(c).wait_recv()

                @pl.when(c >= 2)
                def _():
                    for d in range(1, R):
                        f_copy(c - 2, d, True).wait_send()

                for d in range(1, R):
                    f_copy(c, d, True).start()

        @pl.when((pcol == 0) & (i == panel // width + 4))
        def _():
            for d in range(1, Q):
                g_copy(d).start()

        return carry

    lax.fori_loop(0, K + LAST, body, 0)

    for c in (K - 2, K - 1):
        b_copy(c).wait_send()

        @pl.when(inner)
        def _():
            e_copy(c).wait_send()
            k_copy(c).wait()

            @pl.when(first_rank)
            def _():
                l_copy(c).wait_send()
                lk_copy(c).wait()
                for d in range(1, R):
                    f_copy(c, d, False).wait_send()

        @pl.when(outer & first_rank)
        def _():
            for d in range(1, R):
                f_copy(c, d, True).wait_send()

    @pl.when(outer)
    def _():
        for c in range(K - SLOTS, K):
            c_copy(c).wait_send()

    @pl.when(rank > 0)
    def _():
        @pl.loop(0, K)
        def _(c):
            f_copy(c, 0, True).wait_recv() if R == 1 else f_copy(c, 1, True).wait_recv()

    @pl.when(pcol == 0)
    def _():
        for d in range(1, Q):
            g_copy(d).wait_send()

    @pl.when(pcol > 0)
    def _():
        g_copy(1).wait_recv()


def per_device(system, row_outer, row_inner, col_outer, col_inner, diag_inverse):
    panel = diag_inverse.shape[0]
    rows, cols = system.shape
    R = lax.axis_size("prow") // 4
    Q = lax.axis_size("pcol")
    C = Q // 4
    width = min(WIDTH, panel, cols // 8)
    K = cols // width
    f32, bf16 = jnp.float32, jnp.bfloat16
    assert lax.axis_size("prow") % 4 == 0 and Q % 4 == 0
    assert cols % width == 0 and panel % width == 0 and K >= panel // width + 4
    assert panel <= rows and panel % STRIP == 0 and rows % STRIP == 0
    quarter = lax.axis_index("prow") // R
    col_quarter = lax.axis_index("pcol") // C

    def hops(pairs):
        return [(a * R + r, b * R + r) for a, b in pairs for r in range(R)]

    is1 = quarter == 1
    own = jnp.stack([row_outer, row_inner])
    near = lax.ppermute(own, "prow", hops([(0, 1), (3, 2)]))
    other = lax.ppermute(jnp.concatenate([own, near]), "prow", hops([(1, 2), (2, 1)]))
    across, far = other[:2], other[2:]
    w0 = jnp.where(is1, near, far)
    w1 = jnp.where(is1, own, across)
    w2 = jnp.where(is1, across, own)
    w3 = jnp.where(is1, far, near)
    outer_a, inner_u = jnp.where(is1, w0, w2)
    outer_b, inner_d = jnp.where(is1, w1, w3)
    u0, u1 = 0.5 * inner_u * outer_a, 0.5 * inner_u * outer_b
    d0, d1 = 0.5 * inner_d * outer_a, 0.5 * inner_d * outer_b
    l0, l1 = 0.5 * w0[1] * w0[0], 0.5 * w0[1] * w1[0]
    one = jnp.stack([u1, u0, u0, u1, -d1, d0, d0, -d1, l1, l0, l0, l1])
    two = jnp.stack([-d0, d1, -d1, d0, -u0, -u1, u1, u0, l0, l1, l1, l0])
    row_coef = jnp.where(is1, one, two).T

    outer_c, inner_c = col_outer * root_half, col_inner * root_half
    col_coef = jnp.stack(
        [
            jnp.where(col_quarter < 2, outer_c, -outer_c),
            outer_c,
            jnp.where(col_quarter % 2 == 0, inner_c, -inner_c),
            inner_c,
        ]
    )

    dma = lambda *shape: pltpu.SemaphoreType.DMA(shape)
    block = lambda n, height: pltpu.VMEM((n, height, width), bf16)
    any_spec = pl.BlockSpec(memory_space=pl.ANY)
    vmem_spec = pl.BlockSpec(memory_space=pltpu.VMEM)
    full, lead, leading = pl.pallas_call(
        functools.partial(kernel, K, width, panel, R, Q),
        out_shape=(
            jax.ShapeDtypeStruct((rows, cols), bf16),
            jax.ShapeDtypeStruct((panel, cols), bf16),
            jax.ShapeDtypeStruct((rows, panel), bf16),
        ),
        in_specs=[any_spec, vmem_spec, vmem_spec],
        out_specs=(any_spec, any_spec, any_spec),
        scratch_shapes=[
            block(SLOTS, rows), block(SLOTS, rows), block(2, rows), block(2, rows),
            block(SLOTS, rows), block(SLOTS, rows), block(SLOTS, rows), block(SLOTS, rows),
            block(2, rows), block(2, rows), block(2, panel),
            dma(SLOTS), dma(SLOTS), dma(SLOTS), dma(2), dma(2), dma(SLOTS), dma(SLOTS), dma(SLOTS),
            dma(SLOTS), dma(SLOTS),
            dma(2), dma(K), dma(2), dma(K), dma(2), dma(2), dma(2, max(R - 1, 1)), dma(K), dma(Q - 1), dma(1),
            pltpu.SemaphoreType.REGULAR, pltpu.SemaphoreType.REGULAR,
            pltpu.SemaphoreType.REGULAR, pltpu.SemaphoreType.REGULAR,
        ],
        compiler_params=pltpu.CompilerParams(
            collective_id=0, has_side_effects=True, vmem_limit_bytes=60 * 1024 * 1024
        ),
    )(system, row_coef, col_coef)
    leading = jnp.where(lax.axis_index("pcol") == 0, full[:, :panel], leading)
    left = jnp.dot(leading, diag_inverse, preferred_element_type=f32).astype(bf16)
    update = jnp.dot(left, lead, preferred_element_type=f32)
    return (full.astype(f32) - update).astype(bf16)


def solution(mesh):
    in_specs = (P("prow", "pcol"), P("prow"), P("prow"), P("pcol"), P("pcol"), P())
    out_specs = P("prow", "pcol")
    return jax.shard_map(
        per_device, mesh=mesh, in_specs=in_specs, out_specs=out_specs, check_vma=False
    )
```

time: 2920 us -> 1210 us (0.41)
  waiting for transfers between devices: 2730 us -> 0.01 us
  Pallas kernels: 0 us -> 1170 us
  other arithmetic: 135 us -> 3.54 us
    ppermute x4 -> x2, waiting for transfers between devices: 2190 us -> 0.01 us  [the longest x1 0.01 us: per_device(): near = lax.ppermute(own, 'prow', hops([(0, 1), (3, 2)]))]
    pallas_call x0 -> x1, Pallas kernels: none -> 1170 us  [per_device(): pl.pallas_call(functools.partial(kernel, K, width, panel, R, Q), out_shap...]
    psum x2 -> x0, waiting for transfers between devices: 538 us -> none  [from_root(): return lax.psum(block, axis)]
    convert_element_type x4 -> x0, other arithmetic: 119 us -> none  [combine(): return (weights * summed * root_half).astype(jnp.bfloat16)]
  transfers between devices with their start and end apart: 6 -> 2, of which waited for: 6 -> 0; matrix products, arithmetic and copies ran while one was open for 0% -> 0% of each run, Pallas kernels for 0% -> 0%
where the time goes in v1:
time: 1210 us
  Pallas kernels  1170 us (97%)
  matrix products  27.3 us (2%)
    pallas_call x1, Pallas kernels, per_device(): pl.pallas_call(functools.partial(kernel, K, width, panel, R, Q), out_shap...  1170 us
    dot_general x1, matrix products, per_device(): update = jnp.dot(left, lead, preferred_element_type=f32)  27.3 us
  transfers between devices with their start and end apart: 2, of which 0 were waited for; matrix products, arithmetic and copies ran while one was open for 0% of the time, Pallas kernels for 0%

profile of v1, /device:TPU:7, one launch (start us, length us, event | category | flops | bytes accessed | tf_op | source)
XLA Modules:
  0.0 1205.5 jit_solution(17341331662297268305)
XLA Ops:
  0.0 0.0 copy-start
  0.0 0.7 stack.20
  0.8 0.7 stack.21
  1.5 3.2 collective-permute-start
  4.7 0.9 negate_select_fusion.1
  5.5 0.9 negate_select_fusion
  6.4 0.0 collective-permute-done
  6.4 0.7 collective-permute-start.1
  7.1 1.0 pad_maximum_fusion.col_coef
  8.1 0.0 collective-permute-done.1
  8.1 0.1 stack.23
  8.2 0.2 copy.11
  8.4 0.1 stack.24
  8.5 0.2 copy.12
  8.7 0.8 select_bitcast_fusion.row_coef
  9.4 1168.8 %shard_map.64 = (bf16[768,16384]{1,0:T(8,128)(2,1)}, bf16[512,16384]{1,0:T(8,128)(2,1)}, bf16[768,512]{1,0:T(8,128)(2,1)}) custom-call(bf16[768,16384]{1,0:T(8,128)(2,1)} %system.1, f32[768,12]{1,0:T(8,128)} %select_bitcast_fusion.row_coef, f32[4,16384]{1,0:T(4,128)} %pad_maximum_fusion.col_coef), custom_call_target="tpu_custom_call" | custom-call | tf_op jit(solution)/shard_map/pallas_call | solution.py:361
  1178.2 0.0 copy-done
  1178.2 27.3 %subtract_convert_fusion = bf16[768,16384]{1,0:T(8,128)(2,1)} fusion(bf16[768,16384]{1,0:T(8,128)(2,1)} %get-tuple-element.8, bf16[512,16384]{1,0:T(8,128)(2,1)} %get-tuple-element.10, bf16[512,512]{1,0:T(8,128)(2,1)S(1)} %copy-done, bf16[768,512]{1,0:T(8,128)(2,1)} %get-tuple-element.9, pred[]{:T(512)S(6)} %eq.13), kind=kOutput, calls=%fused_computation | convolution fusion | flops 13326090240 | bytes 69206016 | tf_op jit(solution)/shard_map/dot_general | solution.py:386
  (4 shorter events, 0.1 us)
Async XLA Ops:
  0.0 1178.2 %copy-start = (bf16[512,512]{1,0:T(8,128)(2,1)S(1)}, bf16[512,512]{1,0:T(8,128)(2,1)}, u32[]{:S(2)}) copy-start(bf16[512,512]{1,0:T(8,128)(2,1)} %param.11) | copy-start | bytes 1572868
  1.5 4.9 collective-permute-start
  6.4 1.6 collective-permute-start.1

commit v2 on v1

--- a/solution.py
+++ b/solution.py
@@ -9,7 +9,7 @@
 
 root_half = 0.7071067811865476
 MESH = pl.DeviceIdType.MESH
-WIDTH = 512
+WIDTH = 128
 STRIP = 32
 SLOTS = 4
 LAST = 5

time: 1210 us -> 1160 us (0.959)
  Pallas kernels: 1170 us -> 1120 us
    pallas_call x1, Pallas kernels: 1170 us -> 1120 us  [per_device(): pl.pallas_call(functools.partial(kernel, K, width, panel, R, Q), out_shap...]
where the time goes in v2:
time: 1160 us
  Pallas kernels  1120 us (97%)
  matrix products  27.3 us (2%)
    pallas_call x1, Pallas kernels, per_device(): pl.pallas_call(functools.partial(kernel, K, width, panel, R, Q), out_shap...  1120 us
    dot_general x1, matrix products, per_device(): update = jnp.dot(left, lead, preferred_element_type=f32)  27.3 us
  transfers between devices with their start and end apart: 2, of which 0 were waited for; matrix products, arithmetic and copies ran while one was open for 0% of the time, Pallas kernels for 0%

profile of v2, /device:TPU:7, one launch (start us, length us, event | category | flops | bytes accessed | tf_op | source)
XLA Modules:
  0.0 1157.6 jit_solution(3115851826779890858)
XLA Ops:
  0.0 0.0 copy-start
  0.0 0.7 stack.20
  0.8 0.7 stack.21
  1.5 3.2 collective-permute-start
  4.7 0.9 negate_select_fusion.1
  5.5 0.9 negate_select_fusion
  6.4 0.0 collective-permute-done
  6.4 0.7 collective-permute-start.1
  7.1 1.0 pad_maximum_fusion.col_coef
  8.1 0.0 collective-permute-done.1
  8.1 0.1 stack.23
  8.2 0.2 copy.11
  8.4 0.1 stack.24
  8.5 0.2 copy.12
  8.7 0.8 select_bitcast_fusion.row_coef
  9.4 1120.9 %shard_map.64 = (bf16[768,16384]{1,0:T(8,128)(2,1)}, bf16[512,16384]{1,0:T(8,128)(2,1)}, bf16[768,512]{1,0:T(8,128)(2,1)}) custom-call(bf16[768,16384]{1,0:T(8,128)(2,1)} %system.1, f32[768,12]{1,0:T(8,128)} %select_bitcast_fusion.row_coef, f32[4,16384]{1,0:T(4,128)} %pad_maximum_fusion.col_coef), custom_call_target="tpu_custom_call" | custom-call | tf_op jit(solution)/shard_map/pallas_call | solution.py:361
  1130.3 0.0 copy-done
  1130.3 27.3 %subtract_convert_fusion = bf16[768,16384]{1,0:T(8,128)(2,1)} fusion(bf16[768,16384]{1,0:T(8,128)(2,1)} %get-tuple-element.8, bf16[512,16384]{1,0:T(8,128)(2,1)} %get-tuple-element.10, bf16[512,512]{1,0:T(8,128)(2,1)S(1)} %copy-done, bf16[768,512]{1,0:T(8,128)(2,1)} %get-tuple-element.9, pred[]{:T(512)S(6)} %eq.13), kind=kOutput, calls=%fused_computation | convolution fusion | flops 13326090240 | bytes 69206016 | tf_op jit(solution)/shard_map/dot_general | solution.py:386
  (4 shorter events, 0.1 us)
Async XLA Ops:
  0.0 1130.3 %copy-start = (bf16[512,512]{1,0:T(8,128)(2,1)S(1)}, bf16[512,512]{1,0:T(8,128)(2,1)}, u32[]{:S(2)}) copy-start(bf16[512,512]{1,0:T(8,128)(2,1)} %param.11) | copy-start | bytes 1572868
  1.5 4.9 collective-permute-start
  6.4 1.6 collective-permute-start.1

commit v3 on v2

--- a/solution.py
+++ b/solution.py
@@ -17,12 +17,13 @@
 
 def kernel(
     K, width, panel, R, Q,
-    system, row_coef, col_coef,
+    system, own_w, col_coef,
     full, lead, leading,
     s_buf, ra, tb, rb, m_buf, rc, rd1, rd2, e_buf, k_buf, l_buf,
     load_sem, a_send, a_recv, b_send, b_recv, m_send, c_recv, d1_recv, d2_send, d2_recv,
     e_send, e_recv, l_send, l_recv, k_sem, lk_sem, f_send, f_recv, g_send, g_recv,
     cred_a, cred_b, cred_c, cred_d,
+    near_w, across_w, far_w, w_tile, row_coef, w_send, w_recv,
 ):
     rows = system.shape[0]
     C = Q // 4
@@ -39,6 +40,7 @@
     core_dev = (prow, jnp.where(col_quarter % 2 == 0, pcol + C, pcol - C))
     edge_dev = (jnp.where(quarter % 2 == 0, prow + R, prow - R), pcol)
     mid_dev = ((3 - quarter) * R + rank, pcol)
+    cross_dev = (lax.rem(quarter + 2, 4) * R + rank, pcol)
 
     def signal(sem, device):
         pl.semaphore_signal(sem, inc=1, device_id=device, device_id_type=MESH)
@@ -50,7 +52,8 @@
         signal(barrier, (quarter * R + lax.rem(rank + d, R), pcol))
     signal(barrier, edge_dev)
     signal(barrier, mid_dev)
-    pl.semaphore_wait(barrier, Q - 1 + R - 1 + 2)
+    signal(barrier, cross_dev)
+    pl.semaphore_wait(barrier, Q - 1 + R - 1 + 3)
 
     def at(c):
         return pl.ds(pl.multiple_of(c * width, width), width)
@@ -135,6 +138,44 @@
         load(c).wait()
         a_copy(c).start()
 
+    near_copy = remote(own_w, near_w, w_send.at[0], w_recv.at[0], edge_dev)
+    far_copy = remote(own_w, far_w, w_send.at[1], w_recv.at[1], cross_dev)
+    across_copy = remote(own_w, across_w, w_send.at[2], w_recv.at[2], mid_dev)
+
+    @pl.when(outer)
+    def _():
+        near_copy.start()
+        far_copy.start()
+        near_copy.wait_send()
+        far_copy.wait_send()
+
+    @pl.when(inner)
+    def _():
+        across_copy.start()
+        across_copy.wait()
+        near_copy.wait_recv()
+        far_copy.wait_recv()
+        is1 = quarter == 1
+        w_tile[...] = jnp.zeros_like(w_tile)
+        for j in range(rows // 128):
+            b = slice(j * 128, (j + 1) * 128)
+            level = []
+            for n in range(2):
+                o, e = own_w[n : n + 1, b], near_w[n : n + 1, b]
+                a, f = across_w[n : n + 1, b], far_w[n : n + 1, b]
+                level.append((jnp.where(is1, e, f), jnp.where(is1, o, a), jnp.where(is1, a, o), jnp.where(is1, f, e)))
+            wo, wi = level
+            outer_a, outer_b = jnp.where(is1, wo[0], wo[2]), jnp.where(is1, wo[1], wo[3])
+            inner_u, inner_d = 0.5 * jnp.where(is1, wi[0], wi[2]), 0.5 * jnp.where(is1, wi[1], wi[3])
+            u0, u1 = inner_u * outer_a, inner_u * outer_b
+            d0, d1 = inner_d * outer_a, inner_d * outer_b
+            l0, l1 = 0.5 * wi[0] * wo[0], 0.5 * wi[0] * wo[1]
+            one = (u1, u0, u0, u1, -d1, d0, d0, -d1, l1, l0, l0, l1)
+            two = (-d0, d1, -d1, d0, -u0, -u1, u1, u0, l0, l1, l1, l0)
+            for n in range(12):
+                w_tile[n : n + 1, :] = jnp.where(is1, one[n], two[n])
+            row_coef[b, :] = w_tile[...].T
+
     def body(i, carry):
         @pl.when(i + 3 < K)
         def _():
@@ -319,31 +360,9 @@
     f32, bf16 = jnp.float32, jnp.bfloat16
     assert lax.axis_size("prow") % 4 == 0 and Q % 4 == 0
     assert cols % width == 0 and panel % width == 0 and K >= panel // width + 4
-    assert panel <= rows and panel % STRIP == 0 and rows % STRIP == 0
-    quarter = lax.axis_index("prow") // R
+    assert panel <= rows and panel % STRIP == 0 and rows % STRIP == 0 and rows % 128 == 0
     col_quarter = lax.axis_index("pcol") // C
-
-    def hops(pairs):
-        return [(a * R + r, b * R + r) for a, b in pairs for r in range(R)]
-
-    is1 = quarter == 1
-    own = jnp.stack([row_outer, row_inner])
-    near = lax.ppermute(own, "prow", hops([(0, 1), (3, 2)]))
-    other = lax.ppermute(jnp.concatenate([own, near]), "prow", hops([(1, 2), (2, 1)]))
-    across, far = other[:2], other[2:]
-    w0 = jnp.where(is1, near, far)
-    w1 = jnp.where(is1, own, across)
-    w2 = jnp.where(is1, across, own)
-    w3 = jnp.where(is1, far, near)
-    outer_a, inner_u = jnp.where(is1, w0, w2)
-    outer_b, inner_d = jnp.where(is1, w1, w3)
-    u0, u1 = 0.5 * inner_u * outer_a, 0.5 * inner_u * outer_b
-    d0, d1 = 0.5 * inner_d * outer_a, 0.5 * inner_d * outer_b
-    l0, l1 = 0.5 * w0[1] * w0[0], 0.5 * w0[1] * w1[0]
-    one = jnp.stack([u1, u0, u0, u1, -d1, d0, d0, -d1, l1, l0, l0, l1])
-    two = jnp.stack([-d0, d1, -d1, d0, -u0, -u1, u1, u0, l0, l1, l1, l0])
-    row_coef = jnp.where(is1, one, two).T
-
+    own_w = jnp.concatenate([row_outer[None], row_inner[None], jnp.zeros((6, rows), f32)])
     outer_c, inner_c = col_outer * root_half, col_inner * root_half
     col_coef = jnp.stack(
         [
@@ -376,11 +395,13 @@
             dma(2), dma(K), dma(2), dma(K), dma(2), dma(2), dma(2, max(R - 1, 1)), dma(K), dma(Q - 1), dma(1),
             pltpu.SemaphoreType.REGULAR, pltpu.SemaphoreType.REGULAR,
             pltpu.SemaphoreType.REGULAR, pltpu.SemaphoreType.REGULAR,
+            pltpu.VMEM((8, rows), f32), pltpu.VMEM((8, rows), f32), pltpu.VMEM((8, rows), f32),
+            pltpu.VMEM((128, 128), f32), pltpu.VMEM((rows, 128), f32), dma(3), dma(3),
         ],
         compiler_params=pltpu.CompilerParams(
             collective_id=0, has_side_effects=True, vmem_limit_bytes=60 * 1024 * 1024
         ),
-    )(system, row_coef, col_coef)
+    )(system, own_w, col_coef)
     leading = jnp.where(lax.axis_index("pcol") == 0, full[:, :panel], leading)
     left = jnp.dot(leading, diag_inverse, preferred_element_type=f32).astype(bf16)
     update = jnp.dot(left, lead, preferred_element_type=f32)

time: 1160 us -> 1150 us (level)
  transfers between devices with their start and end apart: 2 -> 0, of which waited for: 0 -> 0; matrix products, arithmetic and copies ran while one was open for 0% -> 0% of each run, Pallas kernels for 0% -> 0%
where the time goes in v3:
time: 1150 us
  Pallas kernels  1120 us (97%)
  matrix products  27.3 us (2%)
    pallas_call x1, Pallas kernels, per_device(): pl.pallas_call(functools.partial(kernel, K, width, panel, R, Q), out_shap...  1120 us
    dot_general x1, matrix products, per_device(): update = jnp.dot(left, lead, preferred_element_type=f32)  27.3 us

profile of v3, /device:TPU:7, one launch (start us, length us, event | category | flops | bytes accessed | tf_op | source)
XLA Modules:
  0.0 1149.5 jit_solution(4128401528903297959)
XLA Ops:
  0.0 0.0 copy-start
  0.0 0.1 pad.6.clone
  0.1 0.7 broadcast_in_dim.9
  0.8 0.7 broadcast_in_dim.10
  1.5 0.7 maximum_maximum_fusion.own_w
  2.2 0.9 negate_select_fusion.1
  3.0 0.9 negate_select_fusion
  3.9 1.0 pad_maximum_fusion.col_coef
  4.8 1117.3 %shard_map.64 = (bf16[768,16384]{1,0:T(8,128)(2,1)}, bf16[512,16384]{1,0:T(8,128)(2,1)}, bf16[768,512]{1,0:T(8,128)(2,1)}) custom-call(bf16[768,16384]{1,0:T(8,128)(2,1)} %system.1, f32[8,768]{1,0:T(8,128)} %maximum_maximum_fusion.own_w, f32[4,16384]{1,0:T(4,128)} %pad_maximum_fusion.col_coef), custom_call_target="tpu_custom_call" | custom-call | tf_op jit(solution)/shard_map/pallas_call | solution.py:380
  1122.2 0.0 copy-done
  1122.2 27.3 %subtract_convert_fusion = bf16[768,16384]{1,0:T(8,128)(2,1)} fusion(bf16[768,16384]{1,0:T(8,128)(2,1)} %get-tuple-element.8, bf16[512,16384]{1,0:T(8,128)(2,1)} %get-tuple-element.10, bf16[512,512]{1,0:T(8,128)(2,1)S(1)} %copy-done, bf16[768,512]{1,0:T(8,128)(2,1)} %get-tuple-element.9, pred[]{:T(512)S(6)} %eq.9), kind=kOutput, calls=%fused_computation | convolution fusion | flops 13326090240 | bytes 69206016 | tf_op jit(solution)/shard_map/dot_general | solution.py:407
  (1 shorter events, 0.0 us)
Async XLA Ops:
  0.0 1122.2 %copy-start = (bf16[512,512]{1,0:T(8,128)(2,1)S(1)}, bf16[512,512]{1,0:T(8,128)(2,1)}, u32[]{:S(2)}) copy-start(bf16[512,512]{1,0:T(8,128)(2,1)} %param.11) | copy-start | bytes 1572868
